TPU v7x, 32 devices: a whole 2x2x4 slice. The times are simulated.
32 devices in a mesh: grp: 2 (over x), row: 16 (over z, y, core).
Axes of the slice: x: 2, y: 2, z: 4, core: 2. Of those that a mesh axis runs over, the one named last changes fastest.
Arguments:
- pair_map: bfloat16 [256, 128, 128], P(('grp', 'row')), parts along dimension 0, may hold values from -6 to 6
- norm_gain: float32 [128], replicated, may hold values from 0.1 to 1.9
- w_query: bfloat16 [128, 128], replicated, may hold values from -30 to 30
- w_key: bfloat16 [128, 128], replicated, may hold values from -1 to 1
- w_value: bfloat16 [128, 128], replicated, may hold values from -0.5 to 0.5
- w_gate: bfloat16 [128, 128], replicated, may hold values from -0.5 to 0.5
- w_bias: bfloat16 [128, 4], replicated, may hold values from -12 to 12
- w_output: bfloat16 [128, 128], replicated, may hold values from -0.5 to 0.5
- window_start: int32 [256], P(('grp', 'row')), parts along dimension 0, may hold values from 0 to 63
- key_length: int32 [256], P(('grp', 'row')), parts along dimension 0, may hold values from 32 to 64
Outputs:
- update: bfloat16 [256, 128, 128], P('grp', 'row'), parts along dimension 0
There are 2 independent parts, one for each index of `grp`. A program takes and returns all parts, laid end to end along the dimension named above; an argument that names none is the same for every part. Nothing has to cross between parts.
All inputs are finite; a program needn't handle non-finite values.
Results may differ from a plain program's by a relative error of at most 0.0025.
The roundings to bfloat16 on the way count: a program that leaves them out, or rounds other values in their place, can miss the bound.
Values may be sent and summed in bfloat16 or wider, within the bound.
A program may use at most 128 MiB of HBM per device.

v0:
```python
import math
import jax
import jax.numpy as jnp
from jax import lax
from jax.sharding import PartitionSpec as P

H = 4


def normalize(rows, norm_gain):
    values = rows.astype(jnp.float32)
    center = jnp.mean(values, axis=-1, keepdims=True)
    spread = jnp.mean((values - center) ** 2, axis=-1, keepdims=True)
    return ((values - center) * lax.rsqrt(spread + 1e-05) * norm_gain).astype(jnp.bfloat16)


def local(
    pair_map, norm_gain, w_query, w_key, w_value, w_gate, w_bias, w_output, window_start, key_length
):
    rows, width, channels = pair_map.shape
    head_size = channels // H
    normed = normalize(pair_map, norm_gain)
    stacked = jnp.concatenate([w_query, w_key, w_value, w_gate], axis=1)
    projected = jnp.dot(
        normed.reshape(rows * width, channels), stacked, preferred_element_type=jnp.float32
    )
    query = projected[:, :channels].astype(jnp.bfloat16).reshape(rows, width, H, head_size)
    key = (
        projected[:, channels : 2 * channels]
        .astype(jnp.bfloat16)
        .reshape(rows, width, H, head_size)
    )
    value = (
        projected[:, 2 * channels : 3 * channels]
        .astype(jnp.bfloat16)
        .reshape(rows, width, H, head_size)
    )
    gate = projected[:, 3 * channels :].astype(jnp.bfloat16).reshape(rows, width, channels)
    local_bias = jnp.einsum("rnc,ch->hrn", normed, w_bias, preferred_element_type=jnp.float32)
    positions = jnp.arange(width, dtype=jnp.int32)
    valid = (positions[None, :] >= window_start[:, None]) & (
        positions[None, :] < (window_start + key_length)[:, None]
    )
    factor = 1.0 / head_size**0.5
    all_bias = lax.all_gather(local_bias, "row", axis=1, tiled=True)
    length = all_bias.shape[1]
    block = math.gcd(length, 64)

    def one_block(index):
        offset = index * block
        bias_block = lax.dynamic_slice_in_dim(all_bias, offset, block, 1)
        query_block = lax.dynamic_slice_in_dim(query, offset, block, 1)
        gate_block = lax.dynamic_slice_in_dim(gate, offset, block, 1)
        scores = (
            jnp.einsum("rjhd,rkhd->rhjk", query_block, key, preferred_element_type=jnp.float32)
            * factor
        )
        scores = scores + bias_block[None]
        scores = jnp.where(valid[:, None, None, :], scores, jnp.float32(-1e30))
        top = jnp.max(scores, axis=-1, keepdims=True)
        raised = jnp.exp(scores - top)
        weights = (raised / jnp.sum(raised, axis=-1, keepdims=True)).astype(jnp.bfloat16)
        attended = jnp.einsum("rhjk,rkhd->rjhd", weights, value, preferred_element_type=jnp.float32)
        attended = attended.reshape(rows, block, channels)
        gated = (jax.nn.sigmoid(gate_block.astype(jnp.float32)) * attended).astype(jnp.bfloat16)
        mixed = jnp.dot(
            gated.reshape(rows * block, channels), w_output, preferred_element_type=jnp.float32
        )
        return mixed.astype(jnp.bfloat16).reshape(rows, block, channels)

    blocks = lax.map(one_block, jnp.arange(length // block, dtype=jnp.int32))
    result = jnp.moveaxis(blocks, 0, 1).reshape(rows, length, channels)
    return lax.all_to_all(result, "row", split_axis=1, concat_axis=0, tiled=True)


def solution(mesh):
    return jax.shard_map(
        local,
        mesh=mesh,
        in_specs=(
            P(("grp", "row"), None, None),
            P(),
            P(),
            P(),
            P(),
            P(),
            P(),
            P(),
            P(("grp", "row")),
            P(("grp", "row")),
        ),
        out_specs=P("grp", "row", None),
        check_vma=False,
    )
```

profile of v0, /device:TPU:0, one launch (start us, length us, event | category | flops | bytes accessed | tf_op | source)
XLA Modules:
  0.0 56.8 jit_solution(8926814176208976086)
XLA Ops:
  0.0 0.0 copy-start
  0.0 0.0 copy-start.5
  0.0 0.0 copy-start.4
  0.0 0.0 copy-start.3
  0.0 0.0 copy-start.2
  0.0 1.1 %convert_reduce_fusion = f32[8,128]{1,0:T(8,128)S(1)} fusion(bf16[8,128,128]{2,1,0:T(8,128)(2,1)} %param.12), kind=kLoop, calls=%fused_computation.24 | loop fusion | flops 261120 | bytes 266240 | tf_op jit(solution)/shard_map/reduce_sum | solution.py:12
  1.2 1.3 %fusion.17 = f32[8,128]{1,0:T(8,128)S(1)} fusion(bf16[8,128,128]{2,1,0:T(8,128)(2,1)} %param.12, f32[8,128]{1,0:T(8,128)S(1)} %broadcast_multiply_fusion), kind=kLoop, calls=%fused_computation.27 | loop fusion | flops 523264 | bytes 270336 | tf_op jit(solution)/shard_map/reduce_sum | solution.py:13
  2.5 1.3 %fusion.19 = bf16[8,128,128]{2,1,0:T(8,128)(2,1)S(1)} fusion(bf16[8,128,128]{2,1,0:T(8,128)(2,1)} %param.12, f32[128]{0:T(128)} %param.13, f32[8,128]{1,0:T(8,128)S(1)} %add_rsqrt_fusion, f32[8,128]{1,0:T(8,128)S(1)} %broadcast_multiply_fusion), kind=kLoop, calls=%fused_computation.29 | loop fusion | flops 655360 | bytes 532992 | tf_op jit(solution)/shard_map/convert_element_type | solution.py:14
  3.8 0.0 copy-done.5
  3.8 0.0 copy-done.4
  3.8 0.0 copy-done.3
  3.9 0.0 copy-done.2
  3.9 0.4 convolution_convert_fusion.1
  4.3 0.2 fusion.32
  4.5 0.1 copy.37
  4.7 0.1 copy.38
  4.9 0.0 copy-start.6
  4.9 0.0 copy-start.7
  5.0 0.0 copy-start.1
  5.0 0.1 copy.36
  5.2 0.0 copy-done
  5.2 0.2 convolution_bitcast_fusion
  5.4 23.8 %all_gather.3 = f32[4,128,128]{2,0,1:T(4,128)S(1)} all-gather(f32[4,8,128]{2,0,1:T(4,128)S(1)} %convolution_bitcast_fusion), channel_id=1, replica_groups=mesh['grp'=2,'row'=16] {'row'}, dimensions={1}, use_global_device_ids=true | all-gather | bytes 278528 | tf_op jit(solution)/shard_map/all_gather | solution.py:45
  29.2 0.0 copy-done.6
  29.2 0.0 copy-done.7
  29.2 0.0 copy-done.1
  29.3 13.9 %while.11 = (s32[]{:T(128)}, bf16[2,8,64,128]{3,2,0,1:T(8,128)(2,1)S(1)}, s32[2]{0:T(128)S(1)}, bf16[8,128,128]{2,1,0:T(8,128)(2,1)S(1)}, bf16[8,128,4,32]{1,0,3...) while((s32[]{:T(128)}, ...), condition=%wide.region_5.6_spmd.clone, body=%wide.region_2.5_spmd.clone.sunk | while | flops 70456576 | bytes 6081815 | solution.py:71
  29.3 0.7 %dynamic_slice.27 = s32[1]{0:T(128)} dynamic-slice(s32[2]{0:T(128)S(1)} %get-tuple-element.253, s32[]{:T(128)} %get-tuple-element.236), dynamic_slice_sizes={1} | dynamic-slice | bytes 12 | tf_op jit(solution)/shard_map/while/body/jit(dynamic_index_in_dim)/dynamic_slice | solution.py:71
  30.6 0.1 constant_dynamic-slice_fusion.5
  30.8 0.1 fusion.61
  30.9 0.3 fusion.63
  31.3 0.8 %fusion.62 = f32[8,4,64]{2,1,0:T(4,128)S(1)} fusion(bf16[8,128,4,32]{1,3,2,0:T(8,128)(2,1)S(1)} %get-tuple-element.256, f32[4,64,128]{2,1,0:T(8,128)S(1)} %copy.67, pred[8,128]{1,0:T(8,128)(4,1)S(1)} %fusion.61, bf16[8,64,4,32]{1,0,3,2:T(8,128)(2,1)S(1)} %constant_dynamic-slice_fusion.5), kind=kOutput, calls=%fused_computation.41.clone.1 | convolution fusion | flops 18088064 | bytes 533504 | tf_op jit(solution)/shard_map/while/body/eval_jaxpr/sub | solution.py:61
  32.1 3.6 %fusion.64 = f32[8,4,64,32]{2,3,1,0:T(8,128)S(1)} fusion(bf16[8,128,4,32]{1,3,2,0:T(8,128)(2,1)S(1)} %get-tuple-element.258, f32[8,4,64]{2,1,0:T(4,128)S(1)} %fusion.62, f32[8,4,64,128]{3,2,1,0:T(8,128)S(1)} %fusion.63), kind=kOutput, calls=%fused_computation.9.clone.1 | convolution fusion | flops 17565824 | bytes 1581056 | tf_op jit(solution)/shard_map/while/body/eval_jaxpr/rhjk,rkhd->rjhd/dot_general | solution.py:63
  35.7 0.2 copy.68
  35.9 0.1 multiply_convert_fusion.2
  36.0 0.2 convolution_convert_fusion.3
  36.2 0.7 %dynamic_slice.27 = s32[1]{0:T(128)} dynamic-slice(s32[2]{0:T(128)S(1)} %get-tuple-element.253, s32[]{:T(128)} %get-tuple-element.236), dynamic_slice_sizes={1} | dynamic-slice | bytes 12 | tf_op jit(solution)/shard_map/while/body/jit(dynamic_index_in_dim)/dynamic_slice | solution.py:71
  37.6 0.1 constant_dynamic-slice_fusion.5
  37.8 0.1 fusion.61
  37.9 0.3 fusion.63
  38.2 0.8 %fusion.62 = f32[8,4,64]{2,1,0:T(4,128)S(1)} fusion(bf16[8,128,4,32]{1,3,2,0:T(8,128)(2,1)S(1)} %get-tuple-element.256, f32[4,64,128]{2,1,0:T(8,128)S(1)} %copy.67, pred[8,128]{1,0:T(8,128)(4,1)S(1)} %fusion.61, bf16[8,64,4,32]{1,0,3,2:T(8,128)(2,1)S(1)} %constant_dynamic-slice_fusion.5), kind=kOutput, calls=%fused_computation.41.clone.1 | convolution fusion | flops 18088064 | bytes 533504 | tf_op jit(solution)/shard_map/while/body/eval_jaxpr/sub | solution.py:61
  39.1 3.6 %fusion.64 = f32[8,4,64,32]{2,3,1,0:T(8,128)S(1)} fusion(bf16[8,128,4,32]{1,3,2,0:T(8,128)(2,1)S(1)} %get-tuple-element.258, f32[8,4,64]{2,1,0:T(4,128)S(1)} %fusion.62, f32[8,4,64,128]{3,2,1,0:T(8,128)S(1)} %fusion.63), kind=kOutput, calls=%fused_computation.9.clone.1 | convolution fusion | flops 17565824 | bytes 1581056 | tf_op jit(solution)/shard_map/while/body/eval_jaxpr/rhjk,rkhd->rjhd/dot_general | solution.py:63
  42.7 0.2 copy.68
  42.9 0.1 multiply_convert_fusion.2
  43.0 0.2 convolution_convert_fusion.3
  43.2 0.2 copy.44
  43.4 12.6 %all_to_all.18 = bf16[8,128,128]{2,0,1:T(8,128)(2,1)S(1)} all-to-all(bf16[8,128,128]{2,0,1:T(8,128)(2,1)S(1)} %copy.44), channel_id=1, replica_groups=mesh['grp'=2,'row'=16] {'row'}, dimensions={1} | all-to-all | bytes 524288 | tf_op jit(solution)/shard_map/all_to_all | solution.py:73
  56.0 0.8 %copy.46 = bf16[16,8,8,128]{3,2,1,0:T(8,128)(2,1)} copy(bf16[16,8,8,128]{3,1,2,0:T(8,128)(2,1)S(1)} %bitcast.76) | data formatting | bytes 524288 | tf_op jit(solution)/shard_map/all_to_all | solution.py:73
  (16 shorter events, 0.3 us)
Async XLA Ops:
  0.0 5.2 %copy-start = (bf16[128,4]{0,1:T(4,128)(2,1)S(1)}, bf16[128,4]{0,1:T(4,128)(2,1)}, u32[]{:S(2)}) copy-start(bf16[128,4]{0,1:T(4,128)(2,1)} %param.18) | copy-start | bytes 3076
  0.0 3.8 %copy-start.5 = (bf16[128,128]{1,0:T(8,128)(2,1)S(1)}, bf16[128,128]{1,0:T(8,128)(2,1)}, u32[]{:S(2)}) copy-start(bf16[128,128]{1,0:T(8,128)(2,1)} %param.14) | copy-start | bytes 98308
  0.0 3.8 %copy-start.4 = (bf16[128,128]{1,0:T(8,128)(2,1)S(1)}, bf16[128,128]{1,0:T(8,128)(2,1)}, u32[]{:S(2)}) copy-start(bf16[128,128]{1,0:T(8,128)(2,1)} %param.15) | copy-start | bytes 98308
  0.0 3.8 %copy-start.3 = (bf16[128,128]{1,0:T(8,128)(2,1)S(1)}, bf16[128,128]{1,0:T(8,128)(2,1)}, u32[]{:S(2)}) copy-start(bf16[128,128]{1,0:T(8,128)(2,1)} %param.16) | copy-start | bytes 98308
  0.0 3.8 %copy-start.2 = (bf16[128,128]{1,0:T(8,128)(2,1)S(1)}, bf16[128,128]{1,0:T(8,128)(2,1)}, u32[]{:S(2)}) copy-start(bf16[128,128]{1,0:T(8,128)(2,1)} %param.17) | copy-start | bytes 98308
  4.9 24.3 %copy-start.6 = (s32[8]{0:T(128)S(1)}, s32[8]{0:T(128)}, u32[]{:S(2)}) copy-start(s32[8]{0:T(128)} %param.20) | copy-start | bytes 100
  4.9 24.3 %copy-start.7 = (s32[8]{0:T(128)S(1)}, s32[8]{0:T(128)}, u32[]{:S(2)}) copy-start(s32[8]{0:T(128)} %param.21) | copy-start | bytes 100
  5.0 24.3 %copy-start.1 = (bf16[128,128]{1,0:T(8,128)(2,1)S(1)}, bf16[128,128]{1,0:T(8,128)(2,1)}, u32[]{:S(2)}) copy-start(bf16[128,128]{1,0:T(8,128)(2,1)} %param.19) | copy-start | bytes 98308
where the time goes:
time: 57 us; the launch traced here: 56.8 us
  blocking collectives  36.4 us (64%)
  matrix products  10.6 us (19%)
  other arithmetic  4.09 us (7%)
  local copies, waits for them, and re-layouts  3.88 us (7%)
  loops' own time  1.56 us (3%)
    all_gather x1, blocking collectives, local(): all_bias = lax.all_gather(local_bias, 'row', axis=1, tiled=True)  23.8 us
    all_to_all x1, blocking collectives, local(): lax.all_to_all(result, 'row', split_axis=1, concat_axis=0, tiled=True)  12.6 us
    dot_general x2, matrix products, one_block(): jnp.einsum('rhjk,rkhd->rjhd', weights, value, preferred_element_type=jnp....  7.26 us
    sub x2, matrix products, one_block(): raised = jnp.exp(scores - top)  1.69 us
    another operation x1, loops' own time, local(): blocks = lax.map(one_block, jnp.arange(length // block, dtype=jnp.int32))  1.56 us
    dynamic_slice x2, local copies, waits for them, and re-layouts, local(): blocks = lax.map(one_block, jnp.arange(length // block, dtype=jnp.int32))  1.33 us
    reduce_sum x1, other arithmetic, normalize(): spread = jnp.mean((values - center) ** 2, axis=-1, keepdims=True)  1.32 us
    convert_element_type x1, other arithmetic, normalize(): ((values - center) * lax.rsqrt(spread + 1e-05) * norm_gain).astype(jnp.bf...  1.29 us

commit v1 on v0

--- a/solution.py
+++ b/solution.py
@@ -42,7 +42,9 @@
         positions[None, :] < (window_start + key_length)[:, None]
     )
     factor = 1.0 / head_size**0.5
-    all_bias = lax.all_gather(local_bias, "row", axis=1, tiled=True)
+    all_bias = jnp.concatenate(
+        lax.all_to_all(jnp.stack([local_bias] * lax.axis_size("row")), "row", 0, 0), axis=1
+    )
     length = all_bias.shape[1]
     block = math.gcd(length, 64)
 

time: 57 us -> 49.9 us (0.88)
  blocking collectives: 36.4 us -> 12.7 us
  waiting for transfers between devices: 0 us -> 8.27 us
  starting transfers between devices: 0 us -> 7.42 us
  local copies, waits for them, and re-layouts: 3.88 us -> 4.81 us
    all_gather x1 -> x0, blocking collectives: 23.8 us -> none  [local(): all_bias = lax.all_gather(local_bias, 'row', axis=1, tiled=True)]
    all_to_all x0 -> x1, waiting for transfers between devices: none -> 8.27 us  [local(): lax.all_to_all(jnp.stack([local_bias] * lax.axis_size('row')), 'row', 0, 0)]
    all_to_all x0 -> x1, starting transfers between devices: none -> 7.42 us  [local(): lax.all_to_all(jnp.stack([local_bias] * lax.axis_size('row')), 'row', 0, 0)]
    another operation x0 -> x1, local copies, waits for them, and re-layouts: none -> 0.75 us  [local(): jnp.stack([local_bias] * lax.axis_size('row'))]
  transfers between devices with their start and end apart: 0 -> 1, of which waited for: 0 -> 1; matrix products, arithmetic and copies ran while one was open for 0% -> 3% of each run, Pallas kernels for 0% -> 0%
where the time goes in v1:
time: 49.9 us; the launch traced here: 49.5 us
  blocking collectives  12.7 us (25%)
  matrix products  10.6 us (21%)
  waiting for transfers between devices  8.27 us (17%)
  starting transfers between devices  7.42 us (15%)
  local copies, waits for them, and re-layouts  4.81 us (10%)
  other arithmetic  4.09 us (8%)
  loops' own time  1.45 us (3%)
    all_to_all x1, blocking collectives, local(): lax.all_to_all(result, 'row', split_axis=1, concat_axis=0, tiled=True)  12.7 us
    all_to_all x1, waiting for transfers between devices, local(): lax.all_to_all(jnp.stack([local_bias] * lax.axis_size('row')), 'row', 0, 0)  8.27 us
    all_to_all x1, starting transfers between devices, local(): lax.all_to_all(jnp.stack([local_bias] * lax.axis_size('row')), 'row', 0, 0)  7.42 us
    dot_general x2, matrix products, one_block(): jnp.einsum('rhjk,rkhd->rjhd', weights, value, preferred_element_type=jnp....  7.26 us
    sub x2, matrix products, one_block(): raised = jnp.exp(scores - top)  1.69 us
    another operation x1, loops' own time, local(): blocks = lax.map(one_block, jnp.arange(length // block, dtype=jnp.int32))  1.45 us
    reduce_sum x1, other arithmetic, normalize(): spread = jnp.mean((values - center) ** 2, axis=-1, keepdims=True)  1.32 us
    convert_element_type x1, other arithmetic, normalize(): ((values - center) * lax.rsqrt(spread + 1e-05) * norm_gain).astype(jnp.bf...  1.29 us
  transfers between devices with their start and end apart: 1, of which 1 were waited for; matrix products, arithmetic and copies ran while one was open for 3% of the time, Pallas kernels for 0%

profile of v1, /device:TPU:0, one launch (start us, length us, event | category | flops | bytes accessed | tf_op | source)
XLA Modules:
  0.0 49.5 jit_solution(5219535996472389857)
XLA Ops:
  0.0 0.0 copy-start
  0.0 0.0 copy-start.5
  0.0 0.0 copy-start.4
  0.0 0.0 copy-start.3
  0.0 0.0 copy-start.2
  0.0 1.1 %convert_reduce_fusion = f32[8,128]{1,0:T(8,128)S(1)} fusion(bf16[8,128,128]{2,1,0:T(8,128)(2,1)} %param.12), kind=kLoop, calls=%fused_computation.24 | loop fusion | flops 261120 | bytes 266240 | tf_op jit(solution)/shard_map/reduce_sum | solution.py:12
  1.2 1.3 %fusion.17 = f32[8,128]{1,0:T(8,128)S(1)} fusion(bf16[8,128,128]{2,1,0:T(8,128)(2,1)} %param.12, f32[8,128]{1,0:T(8,128)S(1)} %broadcast_multiply_fusion), kind=kLoop, calls=%fused_computation.27 | loop fusion | flops 523264 | bytes 270336 | tf_op jit(solution)/shard_map/reduce_sum | solution.py:13
  2.5 1.3 %fusion.19 = bf16[8,128,128]{2,1,0:T(8,128)(2,1)S(1)} fusion(bf16[8,128,128]{2,1,0:T(8,128)(2,1)} %param.12, f32[128]{0:T(128)} %param.13, f32[8,128]{1,0:T(8,128)S(1)} %add_rsqrt_fusion, f32[8,128]{1,0:T(8,128)S(1)} %broadcast_multiply_fusion), kind=kLoop, calls=%fused_computation.29 | loop fusion | flops 655360 | bytes 532992 | tf_op jit(solution)/shard_map/convert_element_type | solution.py:14
  3.8 0.0 copy-done
  3.8 0.2 convolution_bitcast_fusion
  4.0 0.8 %stack.2 = f32[16,4,8,128]{3,2,1,0:T(8,128)} broadcast(f32[4,8,128]{2,1,0:T(8,128)S(1)} %copy.50), dimensions={1,2,3} | broadcast | bytes 278528 | tf_op jit(solution)/shard_map/stack | solution.py:46
  4.7 7.4 %all-to-all-start = ((f32[16,4,8,128]{3,2,1,0:T(8,128)}), f32[16,4,8,128]{3,2,1,0:T(8,128)S(1)}, u32[]{:S(2)}, u32[]{:S(2)}) async-start(f32[16,4,8,128]{3,2,1,0:T(8,128)} %stack.2), calls=%async_computation | async-start | bytes 524288 | tf_op jit(solution)/shard_map/all_to_all | solution.py:46
  12.2 0.0 copy-done.5
  12.2 0.0 copy-done.4
  12.2 0.0 copy-done.3
  12.2 0.0 copy-done.2
  12.2 0.4 convolution_convert_fusion.1
  12.6 0.2 fusion.32
  12.8 0.1 copy.49
  13.1 0.1 copy.52
  13.2 0.0 copy-start.6
  13.3 0.0 copy-start.7
  13.3 0.0 copy-start.1
  13.4 0.1 copy.48
  13.6 0.3 copy-done.6
  13.9 0.0 copy-done.7
  13.9 8.3 %all-to-all-done = f32[16,4,8,128]{3,2,1,0:T(8,128)S(1)} async-done(((f32[16,4,8,128]{3,2,1,0:T(8,128)}), f32[16,4,8,128]{3,2,1,0:T(8,128)S(1)}, u32[]{:S(2)}, u32[]{:S(2)}) %all-to-all-start) | async-done | bytes 262176 | tf_op jit(solution)/shard_map/all_to_all | solution.py:46
  22.2 0.0 copy-done.1
  22.2 13.7 %while.11 = (s32[]{:T(128)}, bf16[2,8,64,128]{3,2,0,1:T(8,128)(2,1)S(1)}, s32[2]{0:T(128)S(1)}, bf16[8,128,128]{2,1,0:T(8,128)(2,1)S(1)}, bf16[8,128,4,32]{1,0,3...) while((s32[]{:T(128)}, ...), condition=%wide.region_5.6_spmd.clone, body=%wide.region_2.5_spmd.clone.sunk | while | flops 70456576 | bytes 5819671 | solution.py:73
  22.2 0.6 %dynamic_slice.27 = s32[1]{0:T(128)} dynamic-slice(s32[2]{0:T(128)S(1)} %get-tuple-element.264, s32[]{:T(128)} %get-tuple-element.247), dynamic_slice_sizes={1} | dynamic-slice | bytes 12 | tf_op jit(solution)/shard_map/while/body/jit(dynamic_index_in_dim)/dynamic_slice | solution.py:73
  23.5 0.1 constant_dynamic-slice_fusion.5
  23.7 0.1 fusion.61
  23.7 0.3 fusion.63
  24.1 0.8 %fusion.62 = f32[8,4,64]{2,1,0:T(4,128)S(1)} fusion(bf16[8,128,4,32]{1,3,2,0:T(8,128)(2,1)S(1)} %get-tuple-element.267, f32[4,64,128]{2,1,0:T(8,128)S(1)} %constant_dynamic-slice_fusion.4, pred[8,128]{1,0:T(8,128)(4,1)S(1)} %fusion.61, bf16[8,64,4,32]{1,0,3,2:T(8,128)(2,1)S(1)} %constant_dynamic-slice_fusion.5), kind=kOutput, calls=%fused_computation.42.clone.1 | convolution fusion | flops 18088064 | bytes 533504 | tf_op jit(solution)/shard_map/while/body/eval_jaxpr/sub | solution.py:63
  24.9 3.6 %fusion.64 = f32[8,4,64,32]{2,3,1,0:T(8,128)S(1)} fusion(bf16[8,128,4,32]{1,3,2,0:T(8,128)(2,1)S(1)} %get-tuple-element.269, f32[8,4,64]{2,1,0:T(4,128)S(1)} %fusion.62, f32[8,4,64,128]{3,2,1,0:T(8,128)S(1)} %fusion.63), kind=kOutput, calls=%fused_computation.9.clone.1 | convolution fusion | flops 17565824 | bytes 1581056 | tf_op jit(solution)/shard_map/while/body/eval_jaxpr/rhjk,rkhd->rjhd/dot_general | solution.py:65
  28.6 0.2 copy.80
  28.8 0.1 multiply_convert_fusion.2
  28.9 0.2 convolution_convert_fusion.3
  29.1 0.6 %dynamic_slice.27 = s32[1]{0:T(128)} dynamic-slice(s32[2]{0:T(128)S(1)} %get-tuple-element.264, s32[]{:T(128)} %get-tuple-element.247), dynamic_slice_sizes={1} | dynamic-slice | bytes 12 | tf_op jit(solution)/shard_map/while/body/jit(dynamic_index_in_dim)/dynamic_slice | solution.py:73
  30.3 0.1 constant_dynamic-slice_fusion.5
  30.5 0.1 fusion.61
  30.6 0.3 fusion.63
  30.9 0.8 %fusion.62 = f32[8,4,64]{2,1,0:T(4,128)S(1)} fusion(bf16[8,128,4,32]{1,3,2,0:T(8,128)(2,1)S(1)} %get-tuple-element.267, f32[4,64,128]{2,1,0:T(8,128)S(1)} %constant_dynamic-slice_fusion.4, pred[8,128]{1,0:T(8,128)(4,1)S(1)} %fusion.61, bf16[8,64,4,32]{1,0,3,2:T(8,128)(2,1)S(1)} %constant_dynamic-slice_fusion.5), kind=kOutput, calls=%fused_computation.42.clone.1 | convolution fusion | flops 18088064 | bytes 533504 | tf_op jit(solution)/shard_map/while/body/eval_jaxpr/sub | solution.py:63
  31.8 3.6 %fusion.64 = f32[8,4,64,32]{2,3,1,0:T(8,128)S(1)} fusion(bf16[8,128,4,32]{1,3,2,0:T(8,128)(2,1)S(1)} %get-tuple-element.269, f32[8,4,64]{2,1,0:T(4,128)S(1)} %fusion.62, f32[8,4,64,128]{3,2,1,0:T(8,128)S(1)} %fusion.63), kind=kOutput, calls=%fused_computation.9.clone.1 | convolution fusion | flops 17565824 | bytes 1581056 | tf_op jit(solution)/shard_map/while/body/eval_jaxpr/rhjk,rkhd->rjhd/dot_general | solution.py:65
  35.4 0.2 copy.80
  35.6 0.1 multiply_convert_fusion.2
  35.7 0.2 convolution_convert_fusion.3
  35.9 0.2 copy.57
  36.1 12.7 %all_to_all.23 = bf16[8,128,128]{2,0,1:T(8,128)(2,1)S(1)} all-to-all(bf16[8,128,128]{2,0,1:T(8,128)(2,1)S(1)} %copy.57), channel_id=1, replica_groups=mesh['grp'=2,'row'=16] {'row'}, dimensions={1} | all-to-all | bytes 524288 | tf_op jit(solution)/shard_map/all_to_all | solution.py:75
  48.8 0.8 %copy.59 = bf16[16,8,8,128]{3,2,1,0:T(8,128)(2,1)} copy(bf16[16,8,8,128]{3,1,2,0:T(8,128)(2,1)S(1)} %bitcast.82) | data formatting | bytes 524288 | tf_op jit(solution)/shard_map/all_to_all | solution.py:75
  (16 shorter events, 0.3 us)
Async XLA Ops:
  0.0 3.8 %copy-start = (bf16[128,4]{0,1:T(4,128)(2,1)S(1)}, bf16[128,4]{0,1:T(4,128)(2,1)}, u32[]{:S(2)}) copy-start(bf16[128,4]{0,1:T(4,128)(2,1)} %param.18) | copy-start | bytes 3076
  0.0 12.2 %copy-start.5 = (bf16[128,128]{1,0:T(8,128)(2,1)S(1)}, bf16[128,128]{1,0:T(8,128)(2,1)}, u32[]{:S(2)}) copy-start(bf16[128,128]{1,0:T(8,128)(2,1)} %param.14) | copy-start | bytes 98308
  0.0 12.2 %copy-start.4 = (bf16[128,128]{1,0:T(8,128)(2,1)S(1)}, bf16[128,128]{1,0:T(8,128)(2,1)}, u32[]{:S(2)}) copy-start(bf16[128,128]{1,0:T(8,128)(2,1)} %param.15) | copy-start | bytes 98308
  0.0 12.2 %copy-start.3 = (bf16[128,128]{1,0:T(8,128)(2,1)S(1)}, bf16[128,128]{1,0:T(8,128)(2,1)}, u32[]{:S(2)}) copy-start(bf16[128,128]{1,0:T(8,128)(2,1)} %param.16) | copy-start | bytes 98308
  0.0 12.2 %copy-start.2 = (bf16[128,128]{1,0:T(8,128)(2,1)S(1)}, bf16[128,128]{1,0:T(8,128)(2,1)}, u32[]{:S(2)}) copy-start(bf16[128,128]{1,0:T(8,128)(2,1)} %param.17) | copy-start | bytes 98308
  4.7 17.4 %all-to-all-start = ((f32[16,4,8,128]{3,2,1,0:T(8,128)}), f32[16,4,8,128]{3,2,1,0:T(8,128)S(1)}, u32[]{:S(2)}, u32[]{:S(2)}) async-start(f32[16,4,8,128]{3,2,1,0:T(8,128)} %stack.2), calls=%async_computation | async-start | bytes 524288 | tf_op jit(solution)/shard_map/all_to_all | solution.py:46
  13.2 0.7 %copy-start.6 = (s32[8]{0:T(128)S(1)}, s32[8]{0:T(128)}, u32[]{:S(2)}) copy-start(s32[8]{0:T(128)} %param.20) | copy-start | bytes 100
  13.3 0.7 %copy-start.7 = (s32[8]{0:T(128)S(1)}, s32[8]{0:T(128)}, u32[]{:S(2)}) copy-start(s32[8]{0:T(128)} %param.21) | copy-start | bytes 100
  13.3 8.9 %copy-start.1 = (bf16[128,128]{1,0:T(8,128)(2,1)S(1)}, bf16[128,128]{1,0:T(8,128)(2,1)}, u32[]{:S(2)}) copy-start(bf16[128,128]{1,0:T(8,128)(2,1)} %param.19) | copy-start | bytes 98308
